TPU v7x, 32 devices: a whole 2x2x4 slice. The times are simulated.
32 devices in a mesh: row: 4 (over x, core), col: 8 (over z, y).
Axes of the slice: x: 2, y: 2, z: 4, core: 2. Of those that a mesh axis runs over, the one named last changes fastest.
Arguments:
- vectors: float32 [16, 4096], P(None, ('row', 'col')), may hold values from -12 to 12, as said below
- diag_energy: float32 [4096], P(('row', 'col')), may hold values from 0.5 to 4
- blocks: float32 [4, 192, 128, 128], P('row', 'col'), may hold values from -0.078125 to 0.078125
- block_row: int32 [4, 192], P('row', 'col'), may hold values from 0 to 7
- block_col: int32 [4, 192], P('row', 'col'), may hold values from 0 to 3
Outputs:
- image: float32 [16, 4096], P(None, ('row', 'col'))
- resid: float32 [16, 4096], P(None, ('row', 'col'))
Inputs may be any that keep to these rules, and one draw needn't show every extreme that they name: `vectors`: each row of X holds independent entries; the Gram matrix X X^T is positive definite.
All inputs are finite; a program needn't handle non-finite values.
Results may differ from a plain program's by a relative error of at most 0.0003.
Values sent between devices are 32-bit elements; how exact they have to be, the bound alone decides.
A program may use at most 64 MiB of HBM per device.

v0:
```python
import functools

import jax
import jax.numpy as jnp
from jax import lax
from jax.experimental import pallas as pl
from jax.experimental.pallas import tpu as pltpu
from jax.sharding import PartitionSpec as P

BLK = 128
DIRECT = 64
F32 = jnp.float32
BF16 = jnp.bfloat16
MESH = pl.DeviceIdType.MESH


def halves(x):
    high = x.astype(BF16)
    return high, (x - high.astype(F32)).astype(BF16)


def add(terms):
    while len(terms) > 1:
        terms = [a + b for a, b in zip(terms[::2], terms[1::2])] + terms[len(terms) & ~1:]
    return terms[0]


def dot_nt(a, b):
    return lax.dot_general(a, b, (((1,), (1,)), ((), ())), preferred_element_type=F32)


def dot_nn(a, b):
    return lax.dot_general(a, b, (((1,), (0,)), ((), ())), preferred_element_type=F32)


def kernel(
    n_row, n_col,
    x_hbm, diag_hbm, rows_hbm, cols_hbm, blocks_hbm,
    out_ref,
    x_ref, diag_ref, rows_ref, cols_ref, tiles, split, col_x, row_x, col_lhs, row_lhs,
    met_out, met_in, p1_out, p1_in, p2_out, p2_in, g1_out, g1_in, g2_out, g2_in,
    load_sem, cx_s, cx_r, rx_s, rx_r, m_s, m_r, p1_s, p1_r, p2_s, p2_r, g1_s, g1_r, g2_s, g2_r,
):
    count = x_ref.shape[0]
    n_blk = tiles.shape[0]
    my_row = lax.axis_index("row")
    my_col = lax.axis_index("col")

    def fan(axis, size, me, source, target, send, recv):
        copies = []
        for d in range(1, size):
            peer = lax.rem(me + d, size)
            copies.append(
                pltpu.make_async_remote_copy(
                    src_ref=source(peer), dst_ref=target(d), send_sem=send.at[d],
                    recv_sem=recv.at[d], device_id={axis: peer}, device_id_type=MESH,
                )
            )
        for copy in copies:
            copy.start()
        return copies

    fan_row = functools.partial(fan, "row", n_row, my_row)
    fan_col = functools.partial(fan, "col", n_col, my_col)

    barrier = pltpu.get_barrier_semaphore()
    for d in range(1, n_col):
        pl.semaphore_signal(
            barrier, inc=1, device_id={"col": lax.rem(my_col + d, n_col)}, device_id_type=MESH
        )
    for d in range(1, n_row):
        pl.semaphore_signal(
            barrier, inc=1, device_id={"row": lax.rem(my_row + d, n_row)}, device_id_type=MESH
        )

    x_load, *small_loads, load = [
        pltpu.make_async_copy(source, target, load_sem.at[at])
        for at, (source, target) in enumerate(
            [(x_hbm, x_ref), (diag_hbm, diag_ref), (rows_hbm, rows_ref), (cols_hbm, cols_ref),
             (blocks_hbm.at[0], tiles)]
        )
    ]
    for copy in [x_load, *small_loads, load]:
        copy.start()
    x_load.wait()
    pl.semaphore_wait(barrier, n_row + n_col - 2)

    upper = my_col // (n_col // 2)
    row_copies = []
    for at in range(1, n_col):
        far = upper * at + (1 - upper) * (n_col - at)
        row_copies.append(
            pltpu.make_async_remote_copy(
                src_ref=x_ref, dst_ref=row_x.at[my_col], send_sem=rx_s.at[far], recv_sem=rx_r.at[far],
                device_id={"col": lax.rem(my_col + far, n_col)}, device_id_type=MESH,
            )
        )
    for copy in row_copies:
        copy.start()
    col_copies = fan_row(lambda peer: x_ref, lambda d: col_x.at[my_row], cx_s, cx_r)
    x_own = x_ref[...]
    row_x[my_col] = x_own
    col_x[my_row] = x_own

    for copy in [*small_loads, load]:
        copy.wait()
    for b in range(n_blk):
        high, low = halves(tiles[b])
        split[b] = jnp.concatenate([high, low], axis=1)

    per = BLK // count
    groups = count // 8
    lane = lax.broadcasted_iota(jnp.int32, (count, BLK), 1)
    sub = lax.broadcasted_iota(jnp.int32, (count, BLK), 0)
    keep = (lane // count) == (sub % per)

    def fold(o):
        return o[:count, :count] + o[count:, :count] + o[:count, count:]

    def pack(square):
        spread = jnp.where(keep, jnp.concatenate([square] * per, axis=1), 0.0)
        return jnp.concatenate(
            [jnp.sum(spread[g * per:(g + 1) * per], axis=0, keepdims=True) for g in range(groups)], axis=0
        )

    def unpack(packed):
        wide = jnp.concatenate(
            [jnp.broadcast_to(packed[g:g + 1], (per, BLK)) for g in range(groups)], axis=0
        )
        return jnp.where(keep, wide, 0.0)

    for copy in col_copies:
        copy.wait()
    zero = jnp.zeros((count, BLK), BF16)
    col_two = []
    for q in range(n_row):
        high, low = halves(col_x[q])
        col_lhs[q] = jnp.concatenate(
            [jnp.concatenate([high, high], axis=1), jnp.concatenate([low, zero], axis=1)], axis=0
        )
        col_two.append(jnp.concatenate([high, low], axis=0))
    x_wide = jnp.concatenate(col_two, axis=1)
    met_out[...] = pack(fold(dot_nt(x_wide, x_wide)))
    met_copies = fan_col(lambda peer: met_out, lambda d: met_in.at[d], m_s, m_r)

    part_one = [jnp.zeros((count, BLK), F32) for _ in range(n_col)]
    for b in range(n_blk):
        o = dot_nt(col_lhs[cols_ref[0, b]], split[b])
        term = o[:count] + o[count:]
        place = rows_ref[0, b]
        for r in range(n_col):
            part_one[r] = part_one[r] + (place == r).astype(F32) * term
    for r in range(n_col):
        p1_out[r] = part_one[r]
    p1_copies = fan_col(lambda peer: p1_out.at[peer], lambda d: p1_in.at[d], p1_s, p1_r)

    own_diag = diag_ref[...] * x_own
    x_two = jnp.concatenate(halves(x_own), axis=0)
    d_two = jnp.concatenate(halves(own_diag), axis=0)

    sum_two = dot_nt(x_two, d_two)

    def take(at, both):
        row_lhs[at] = both
        p_here = jnp.concatenate(halves(p1_out[at]), axis=0)
        return dot_nt(jnp.concatenate([both, p_here], axis=1), jnp.concatenate([p_here, both], axis=1))

    sum_two = sum_two + take(my_col, x_two)
    for copy_at in range(1, n_col):
        row_copies[copy_at - 1].wait()
        far = upper * copy_at + (1 - upper) * (n_col - copy_at)
        at = lax.rem(my_col - far + n_col, n_col)
        sum_two = sum_two + take(at, jnp.concatenate(halves(row_x[at]), axis=0))
    gram_part = fold(sum_two)
    g1_out[...] = pack(gram_part)
    direct = n_row * n_col <= DIRECT
    if direct:
        g1_copies = []
        for at in range(1, n_col + 1):
            for over in sorted(range(n_row), key=lambda o: abs(2 * o - n_row)):
                if at == n_col and over == 0:
                    continue
                far = lax.rem(upper * at + (1 - upper) * (n_col - at), n_col)
                slot = over * n_col + far
                peer = {"row": lax.rem(my_row + over, n_row), "col": lax.rem(my_col + far, n_col)}
                g1_copies.append(
                    pltpu.make_async_remote_copy(
                        src_ref=g1_out, dst_ref=g1_in.at[slot], send_sem=g1_s.at[slot],
                        recv_sem=g1_r.at[slot], device_id=peer, device_id_type=MESH,
                    )
                )
        for copy in g1_copies:
            copy.start()
    else:
        g1_copies = fan_row(lambda peer: g1_out, lambda d: g1_in.at[d], g1_s, g1_r)

    part_two = [jnp.zeros((count, BLK), F32) for _ in range(n_row)]
    for b in range(n_blk):
        o = dot_nn(row_lhs[rows_ref[0, b]], split[b])
        term = o[:count, :BLK] + o[count:, :BLK] + o[:count, BLK:]
        place = cols_ref[0, b]
        for q in range(n_row):
            part_two[q] = part_two[q] + (place == q).astype(F32) * term
    for q in range(n_row):
        p2_out[q] = part_two[q]
    p2_copies = fan_row(lambda peer: p2_out.at[peer], lambda d: p2_in.at[d], p2_s, p2_r)

    if not direct:
        for copy in g1_copies:
            copy.wait()
        g2_out[...] = add([g1_out[...]] + [g1_in[d] for d in range(1, n_row)])
        g2_copies = fan_col(lambda peer: g2_out, lambda d: g2_in.at[d], g2_s, g2_r)

    for copy in met_copies:
        copy.wait()
    metric = unpack(add([met_out[...]] + [met_in[d] for d in range(1, n_col)]))
    shift = count
    while shift < BLK:
        metric = metric + pltpu.roll(metric, shift, 1)
        shift *= 2
    lines = [jnp.broadcast_to(metric[:, k:k + 1], (count, BLK)) for k in range(count)]
    solved = x_own
    pivots = jnp.ones((count, BLK), F32)
    for k in range(count):
        pivot = lines[k][k:k + 1]
        pivots = jnp.where(sub == k, pivot, pivots)
        ratio = jnp.where(sub == k, 0.0, lines[k] / pivot)
        solved = solved - ratio * solved[k:k + 1]
        for j in range(k + 1, count):
            lines[j] = lines[j] - ratio * lines[j][k:k + 1]
    high, low = halves(solved / pivots)
    y_two = jnp.concatenate(
        [jnp.concatenate([high] * per, axis=0), jnp.concatenate([low] * per, axis=0)], axis=1
    )

    for copy in p2_copies:
        copy.wait()
    image = own_diag + p2_out[my_row]
    for d in range(1, n_row):
        image = image + p2_in[d]
    for copy in p1_copies:
        copy.wait()
    image = add([image, p1_out[my_col]] + [p1_in[d] for d in range(1, n_col)])
    out_ref[0] = image

    for copy in g1_copies if direct else g2_copies:
        copy.wait()
    if direct:
        gram = add([g1_out[...]] + [g1_in[d] for d in range(1, n_row * n_col)])
    else:
        gram = add([g2_out[...]] + [g2_in[d] for d in range(1, n_col)])
    wide = unpack(gram)
    o = dot_nn(jnp.concatenate(halves(wide), axis=0), y_two)
    out_ref[1] = image - (o[:count, :BLK] + o[count:, :BLK] + o[:count, BLK:])


def part_kernel(both_ref, image_ref, resid_ref):
    image_ref[...] = both_ref[0]
    resid_ref[...] = both_ref[1]


def per_device(n_row, n_col, vectors, diag_energy, blocks, block_row, block_col):
    count = vectors.shape[0]
    n_blk = blocks.shape[1]
    groups = count // 8
    piece = (count, BLK)
    n_all = n_row * n_col if n_row * n_col <= DIRECT else n_row
    vmem = pl.BlockSpec(memory_space=pltpu.VMEM)
    dma = pltpu.SemaphoreType.DMA
    both = pl.pallas_call(
        functools.partial(kernel, n_row, n_col),
        out_shape=pltpu.VMEM((2,) + piece, F32),
        in_specs=[pl.BlockSpec(memory_space=pl.ANY)] * 5,
        out_specs=vmem,
        scratch_shapes=[
            pltpu.VMEM(piece, F32),
            pltpu.VMEM((1, BLK), F32),
            pltpu.SMEM((1, n_blk), jnp.int32),
            pltpu.SMEM((1, n_blk), jnp.int32),
            pltpu.VMEM((n_blk, BLK, BLK), F32),
            pltpu.VMEM((n_blk, BLK, 2 * BLK), BF16),
            pltpu.VMEM((n_row,) + piece, F32),
            pltpu.VMEM((n_col,) + piece, F32),
            pltpu.VMEM((n_row, 2 * count, 2 * BLK), BF16),
            pltpu.VMEM((n_col, 2 * count, BLK), BF16),
            pltpu.VMEM((groups, BLK), F32),
            pltpu.VMEM((n_col, groups, BLK), F32),
            pltpu.VMEM((n_col,) + piece, F32),
            pltpu.VMEM((n_col,) + piece, F32),
            pltpu.VMEM((n_row,) + piece, F32),
            pltpu.VMEM((n_row,) + piece, F32),
            pltpu.VMEM((groups, BLK), F32),
            pltpu.VMEM((n_all, groups, BLK), F32),
            pltpu.VMEM((groups, BLK), F32),
            pltpu.VMEM((n_col, groups, BLK), F32),
            dma((5,)),
            dma((n_row,)), dma((n_row,)),
            dma((n_col,)), dma((n_col,)),
            dma((n_col,)), dma((n_col,)),
            dma((n_col,)), dma((n_col,)),
            dma((n_row,)), dma((n_row,)),
            dma((n_all,)), dma((n_all,)),
            dma((n_col,)), dma((n_col,)),
        ],
        compiler_params=pltpu.CompilerParams(collective_id=0, has_side_effects=True),
    )(vectors, diag_energy.reshape(1, -1), block_row, block_col, blocks)
    return pl.pallas_call(
        part_kernel,
        out_shape=[jax.ShapeDtypeStruct(piece, F32)] * 2,
        in_specs=[vmem],
        out_specs=[vmem, vmem],
    )(pltpu.with_memory_space_constraint(both, pltpu.VMEM))


def solution(mesh):
    return jax.shard_map(
        functools.partial(per_device, mesh.shape["row"], mesh.shape["col"]),
        mesh=mesh,
        in_specs=(
            P(None, ("row", "col")),
            P(("row", "col")),
            P("row", "col", None, None),
            P("row", "col"),
            P("row", "col"),
        ),
        out_specs=(P(None, ("row", "col")), P(None, ("row", "col"))),
        check_vma=False,
    )
```

profile of v0, /device:TPU:0, one launch (start us, length us, event | category | flops | bytes accessed | tf_op | source)
XLA Modules:
  0.0 17.9 jit_solution(3665340329916433962)
XLA Ops:
  0.6 16.7 %shard_map.68.both_ref = f32[2,16,128]{2,1,0:T(8,128)S(1)} custom-call(f32[16,128]{1,0:T(8,128)} %x_hbm.1, f32[1,128]{1,0:T(1,128)} %bitcast.1, s32[1,24]{1,0:T(1,128)} %rows_hbm.1, s32[1,24]{1,0:T(1,128)} %cols_hbm.1, f32[1,24,128,128]{3,2,1,0:T(8,128)} %blocks_hbm.1), custom_call_target="tpu_custom_call" | custom-call | tf_op jit(solution)/shard_map/pallas_call | solution.py:270
  17.3 0.6 %shard_map.69 = (f32[16,128]{1,0:T(8,128)}, f32[16,128]{1,0:T(8,128)}) custom-call(f32[2,16,128]{2,1,0:T(8,128)S(1)} %shard_map.68.both_ref), custom_call_target="tpu_custom_call" | custom-call | tf_op jit(solution)/shard_map/pallas_call | solution.py:307
where the time goes:
time: 18.1 us; the launch traced here: 17.9 us
  Pallas kernels  17.3 us (96%)
  between operations  0.64 us (4%)
    pallas_call x1, Pallas kernels, per_device(): pl.pallas_call(functools.partial(kernel, n_row, n_col), out_shape=pltpu.V...  16.7 us
    pallas_call x1, Pallas kernels, per_device(): pl.pallas_call(part_kernel, out_shape=[jax.ShapeDtypeStruct(piece, F32)]...  0.61 us

commit v1 on v0

v1 whole, which is shorter than its diff:
```python
import functools

import jax
import jax.numpy as jnp
from jax import lax
from jax.experimental import pallas as pl
from jax.experimental.pallas import tpu as pltpu
from jax.sharding import PartitionSpec as P

BLK = 128
DIRECT = 64
F32 = jnp.float32
BF16 = jnp.bfloat16
MESH = pl.DeviceIdType.MESH


def halves(x):
    high = x.astype(BF16)
    return high, (x - high.astype(F32)).astype(BF16)


def add(terms):
    while len(terms) > 1:
        terms = [a + b for a, b in zip(terms[::2], terms[1::2])] + terms[len(terms) & ~1:]
    return terms[0]


def dot_nt(a, b):
    return lax.dot_general(a, b, (((1,), (1,)), ((), ())), preferred_element_type=F32)


def dot_nn(a, b):
    return lax.dot_general(a, b, (((1,), (0,)), ((), ())), preferred_element_type=F32)


def drain(ref, sem):
    pltpu.make_async_copy(ref, ref, sem).wait()


def kernel(
    n_row, n_col,
    x_hbm, diag_hbm, rows_hbm, cols_hbm, blocks_hbm,
    out_ref,
    x_ref, diag_ref, rows_ref, cols_ref, tiles, split, col_x, row_x, col_lhs, row_lhs,
    met_in, p1_out, p1_in, p2_out, p2_in, g1_out, g1_in, g2_out, g2_in, sent,
    load_sem, send, cx_r, rx_r, m_r, p1_r, p2_r, g1_r, g2_r,
):
    count = x_ref.shape[0]
    n_blk = tiles.shape[0]
    my_row = lax.axis_index("row")
    my_col = lax.axis_index("col")
    direct = n_row * n_col <= DIRECT

    def push(source, target, recv, peer):
        pltpu.make_async_remote_copy(
            src_ref=source, dst_ref=target, send_sem=send, recv_sem=recv,
            device_id=peer, device_id_type=MESH,
        ).start()

    def others(size, me):
        return [lax.rem(me + d, size) for d in range(1, size)]

    barrier = pltpu.get_barrier_semaphore()
    for peer in others(n_col, my_col):
        pl.semaphore_signal(barrier, inc=1, device_id={"col": peer}, device_id_type=MESH)
    for peer in others(n_row, my_row):
        pl.semaphore_signal(barrier, inc=1, device_id={"row": peer}, device_id_type=MESH)

    x_load, *small_loads, load = [
        pltpu.make_async_copy(source, target, load_sem.at[at])
        for at, (source, target) in enumerate(
            [(x_hbm, x_ref), (diag_hbm, diag_ref), (rows_hbm, rows_ref), (cols_hbm, cols_ref),
             (blocks_hbm.at[0], tiles)]
        )
    ]
    for copy in [x_load, *small_loads, load]:
        copy.start()
    x_load.wait()
    pl.semaphore_wait(barrier, n_row + n_col - 2)

    upper = my_col // (n_col // 2)
    for at in range(1, n_col):
        far = upper * at + (1 - upper) * (n_col - at)
        push(x_ref, row_x.at[my_col], rx_r, {"col": lax.rem(my_col + far, n_col)})
    for peer in others(n_row, my_row):
        push(x_ref, col_x.at[my_row], cx_r, {"row": peer})
    x_own = x_ref[...]
    row_x[my_col] = x_own
    col_x[my_row] = x_own

    for copy in [*small_loads, load]:
        copy.wait()
    for b in range(n_blk):
        high, low = halves(tiles[b])
        split[b] = jnp.concatenate([high, low], axis=1)

    per = BLK // count
    groups = count // 8
    lane = lax.broadcasted_iota(jnp.int32, (count, BLK), 1)
    sub = lax.broadcasted_iota(jnp.int32, (count, BLK), 0)
    keep = (lane // count) == (sub % per)

    def fold(o):
        return o[:count, :count] + o[count:, :count] + o[:count, count:]

    def pack(square):
        spread = jnp.where(keep, jnp.concatenate([square] * per, axis=1), 0.0)
        return jnp.concatenate(
            [jnp.sum(spread[g * per:(g + 1) * per], axis=0, keepdims=True) for g in range(groups)], axis=0
        )

    def unpack(packed):
        wide = jnp.concatenate(
            [jnp.broadcast_to(packed[g:g + 1], (per, BLK)) for g in range(groups)], axis=0
        )
        return jnp.where(keep, wide, 0.0)

    drain(col_x.at[pl.ds(0, n_row - 1)], cx_r)
    zero = jnp.zeros((count, BLK), BF16)
    col_two = []
    for q in range(n_row):
        high, low = halves(col_x[q])
        col_lhs[q] = jnp.concatenate(
            [jnp.concatenate([high, high], axis=1), jnp.concatenate([low, zero], axis=1)], axis=0
        )
        col_two.append(jnp.concatenate([high, low], axis=0))
    x_wide = jnp.concatenate(col_two, axis=1)
    met_in[my_col] = pack(fold(dot_nt(x_wide, x_wide)))
    for peer in others(n_col, my_col):
        push(met_in.at[my_col], met_in.at[my_col], m_r, {"col": peer})

    part_one = [jnp.zeros((count, BLK), F32) for _ in range(n_col)]
    for b in range(n_blk):
        o = dot_nt(col_lhs[cols_ref[0, b]], split[b])
        term = o[:count] + o[count:]
        place = rows_ref[0, b]
        for r in range(n_col):
            part_one[r] = part_one[r] + (place == r).astype(F32) * term
    for r in range(n_col):
        p1_out[r] = part_one[r]
    for d, peer in enumerate(others(n_col, my_col)):
        push(p1_out.at[peer], p1_in.at[d], p1_r, {"col": peer})

    own_diag = diag_ref[...] * x_own
    left = [jnp.concatenate(halves(x_own), axis=0)]
    right = [jnp.concatenate(halves(own_diag), axis=0)]
    p_two = [jnp.concatenate(halves(part), axis=0) for part in part_one]

    drain(row_x.at[pl.ds(0, n_col - 1)], rx_r)
    for at in range(n_col):
        both = jnp.concatenate(halves(row_x[at]), axis=0)
        row_lhs[at] = both
        left += [both, p_two[at]]
        right += [p_two[at], both]
    packed = pack(fold(dot_nt(jnp.concatenate(left, axis=1), jnp.concatenate(right, axis=1))))
    if direct:
        me = my_col * n_row + my_row
        g1_in[me] = packed
        for at in range(n_row * n_col - 1):
            to = at + (at >= me).astype(jnp.int32)
            push(
                g1_in.at[me], g1_in.at[me], g1_r,
                {"row": lax.rem(to, n_row), "col": to // n_row},
            )
    else:
        g1_out[...] = packed
        for d, peer in enumerate(others(n_row, my_row)):
            push(g1_out, g1_in.at[d], g1_r, {"row": peer})

    part_two = [jnp.zeros((count, BLK), F32) for _ in range(n_row)]
    for b in range(n_blk):
        o = dot_nn(row_lhs[rows_ref[0, b]], split[b])
        term = o[:count, :BLK] + o[count:, :BLK] + o[:count, BLK:]
        place = cols_ref[0, b]
        for q in range(n_row):
            part_two[q] = part_two[q] + (place == q).astype(F32) * term
    for q in range(n_row):
        p2_out[q] = part_two[q]
    for d, peer in enumerate(others(n_row, my_row)):
        push(p2_out.at[peer], p2_in.at[d], p2_r, {"row": peer})

    if not direct:
        drain(g1_in.at[pl.ds(0, n_row - 1)], g1_r)
        g2_out[...] = add([g1_out[...]] + [g1_in[d] for d in range(n_row - 1)])
        for d, peer in enumerate(others(n_col, my_col)):
            push(g2_out, g2_in.at[d], g2_r, {"col": peer})

    drain(met_in.at[pl.ds(0, n_col - 1)], m_r)
    metric = unpack(add([met_in[d] for d in range(n_col)]))
    shift = count
    while shift < BLK:
        metric = metric + pltpu.roll(metric, shift, 1)
        shift *= 2
    lines = [jnp.broadcast_to(metric[:, k:k + 1], (count, BLK)) for k in range(count)]
    solved = x_own
    pivots = jnp.ones((count, BLK), F32)
    for k in range(count):
        pivot = lines[k][k:k + 1]
        pivots = jnp.where(sub == k, pivot, pivots)
        ratio = jnp.where(sub == k, 0.0, lines[k] / pivot)
        solved = solved - ratio * solved[k:k + 1]
        for j in range(k + 1, count):
            lines[j] = lines[j] - ratio * lines[j][k:k + 1]
    high, low = halves(solved / pivots)
    y_two = jnp.concatenate(
        [jnp.concatenate([high] * per, axis=0), jnp.concatenate([low] * per, axis=0)], axis=1
    )

    drain(p2_in.at[pl.ds(0, n_row - 1)], p2_r)
    image = own_diag + p2_out[my_row]
    for d in range(n_row - 1):
        image = image + p2_in[d]
    drain(p1_in.at[pl.ds(0, n_col - 1)], p1_r)
    image = add([image, p1_out[my_col]] + [p1_in[d] for d in range(n_col - 1)])
    out_ref[0] = image

    if direct:
        drain(g1_in.at[pl.ds(0, n_row * n_col - 1)], g1_r)
        gram = add([g1_in[d] for d in range(n_row * n_col)])
    else:
        drain(g2_in.at[pl.ds(0, n_col - 1)], g2_r)
        gram = add([g2_out[...]] + [g2_in[d] for d in range(n_col - 1)])
    wide = unpack(gram)
    o = dot_nn(jnp.concatenate(halves(wide), axis=0), y_two)
    out_ref[1] = image - (o[:count, :BLK] + o[count:, :BLK] + o[:count, BLK:])
    drain(sent, send)


def part_kernel(both_ref, image_ref, resid_ref):
    image_ref[...] = both_ref[0]
    resid_ref[...] = both_ref[1]


def per_device(n_row, n_col, vectors, diag_energy, blocks, block_row, block_col):
    count = vectors.shape[0]
    n_blk = blocks.shape[1]
    groups = count // 8
    piece = (count, BLK)
    direct = n_row * n_col <= DIRECT
    n_all = n_row * n_col if direct else n_row
    pieces = 2 * (n_row + n_col - 2)
    small = n_col - 1 + n_all - 1 + (0 if direct else n_col - 1)
    vmem = pl.BlockSpec(memory_space=pltpu.VMEM)
    dma = pltpu.SemaphoreType.DMA
    both = pl.pallas_call(
        functools.partial(kernel, n_row, n_col),
        out_shape=pltpu.VMEM((2,) + piece, F32),
        in_specs=[pl.BlockSpec(memory_space=pl.ANY)] * 5,
        out_specs=vmem,
        scratch_shapes=[
            pltpu.VMEM(piece, F32),
            pltpu.VMEM((1, BLK), F32),
            pltpu.SMEM((1, n_blk), jnp.int32),
            pltpu.SMEM((1, n_blk), jnp.int32),
            pltpu.VMEM((n_blk, BLK, BLK), F32),
            pltpu.VMEM((n_blk, BLK, 2 * BLK), BF16),
            pltpu.VMEM((n_row,) + piece, F32),
            pltpu.VMEM((n_col,) + piece, F32),
            pltpu.VMEM((n_row, 2 * count, 2 * BLK), BF16),
            pltpu.VMEM((n_col, 2 * count, BLK), BF16),
            pltpu.VMEM((n_col, groups, BLK), F32),
            pltpu.VMEM((n_col,) + piece, F32),
            pltpu.VMEM((n_col - 1,) + piece, F32),
            pltpu.VMEM((n_row,) + piece, F32),
            pltpu.VMEM((n_row - 1,) + piece, F32),
            pltpu.VMEM((groups, BLK), F32),
            pltpu.VMEM((n_all, groups, BLK), F32),
            pltpu.VMEM((groups, BLK), F32),
            pltpu.VMEM((n_col, groups, BLK), F32),
            pltpu.VMEM((8 * pieces + small, groups, BLK), F32),
            dma((5,)),
            dma, dma, dma, dma, dma, dma, dma, dma,
        ],
        compiler_params=pltpu.CompilerParams(collective_id=0, has_side_effects=True),
    )(vectors, diag_energy.reshape(1, -1), block_row, block_col, blocks)
    return pl.pallas_call(
        part_kernel,
        out_shape=[jax.ShapeDtypeStruct(piece, F32)] * 2,
        in_specs=[vmem],
        out_specs=[vmem, vmem],
    )(pltpu.with_memory_space_constraint(both, pltpu.VMEM))


def solution(mesh):
    return jax.shard_map(
        functools.partial(per_device, mesh.shape["row"], mesh.shape["col"]),
        mesh=mesh,
        in_specs=(
            P(None, ("row", "col")),
            P(("row", "col")),
            P("row", "col", None, None),
            P("row", "col"),
            P("row", "col"),
        ),
        out_specs=(P(None, ("row", "col")), P(None, ("row", "col"))),
        check_vma=False,
    )
```

time: 18.1 us -> 17 us (0.939)
  Pallas kernels: 17.3 us -> 16.1 us
    pallas_call x1, Pallas kernels: 16.7 us -> 15.5 us  [per_device(): pl.pallas_call(functools.partial(kernel, n_row, n_col), out_shape=pltpu.V...]
where the time goes in v1:
time: 17 us; the launch traced here: 16.8 us
  Pallas kernels  16.1 us (95%)
  between operations  0.64 us (4%)
    pallas_call x1, Pallas kernels, per_device(): pl.pallas_call(functools.partial(kernel, n_row, n_col), out_shape=pltpu.V...  15.5 us
    pallas_call x1, Pallas kernels, per_device(): pl.pallas_call(part_kernel, out_shape=[jax.ShapeDtypeStruct(piece, F32)]...  0.61 us

profile of v1, /device:TPU:0, one launch (start us, length us, event | category | flops | bytes accessed | tf_op | source)
XLA Modules:
  0.0 16.8 jit_solution(10049117701523862613)
XLA Ops:
  0.6 15.5 %shard_map.68.both_ref = f32[2,16,128]{2,1,0:T(8,128)S(1)} custom-call(f32[16,128]{1,0:T(8,128)} %x_hbm.1, f32[1,128]{1,0:T(1,128)} %bitcast.1, s32[1,24]{1,0:T(1,128)} %rows_hbm.1, s32[1,24]{1,0:T(1,128)} %cols_hbm.1, f32[1,24,128,128]{3,2,1,0:T(8,128)} %blocks_hbm.1), custom_call_target="tpu_custom_call" | custom-call | tf_op jit(solution)/shard_map/pallas_call | solution.py:245
  16.1 0.6 %shard_map.69 = (f32[16,128]{1,0:T(8,128)}, f32[16,128]{1,0:T(8,128)}) custom-call(f32[2,16,128]{2,1,0:T(8,128)S(1)} %shard_map.68.both_ref), custom_call_target="tpu_custom_call" | custom-call | tf_op jit(solution)/shard_map/pallas_call | solution.py:276

commit v2 on v1

--- a/solution.py
+++ b/solution.py
@@ -9,6 +9,7 @@
 
 BLK = 128
 DIRECT = 64
+FAST = 2
 F32 = jnp.float32
 BF16 = jnp.bfloat16
 MESH = pl.DeviceIdType.MESH
@@ -42,8 +43,8 @@
     x_hbm, diag_hbm, rows_hbm, cols_hbm, blocks_hbm,
     out_ref,
     x_ref, diag_ref, rows_ref, cols_ref, tiles, split, col_x, row_x, col_lhs, row_lhs,
-    met_in, p1_out, p1_in, p2_out, p2_in, g1_out, g1_in, g2_out, g2_in, sent,
-    load_sem, send, cx_r, rx_r, m_r, p1_r, p2_r, g1_r, g2_r,
+    met_in, p1_out, p1_in, p2_out, p2_in, g1_out, g1_in, g2_out, g2_in, sent, far_p1, far_g, far_sum,
+    load_sem, send, cx_r, rx_r, m_r, p1_r, p2_r, g1_r, g2_r, far_s, far_r,
 ):
     count = x_ref.shape[0]
     n_blk = tiles.shape[0]
@@ -51,9 +52,12 @@
     my_col = lax.axis_index("col")
     direct = n_row * n_col <= DIRECT
 
-    def push(source, target, recv, peer):
+    last = my_col == n_col - 1
+    first = (my_col == 0) & (my_row < FAST)
+
+    def push(source, target, recv, peer, sem=send):
         pltpu.make_async_remote_copy(
-            src_ref=source, dst_ref=target, send_sem=send, recv_sem=recv,
+            src_ref=source, dst_ref=target, send_sem=sem, recv_sem=recv,
             device_id=peer, device_id_type=MESH,
         ).start()
 
@@ -78,10 +82,12 @@
     x_load.wait()
     pl.semaphore_wait(barrier, n_row + n_col - 2)
 
+    mirror = n_col - 1 - my_col
     upper = my_col // (n_col // 2)
     for at in range(1, n_col):
         far = upper * at + (1 - upper) * (n_col - at)
-        push(x_ref, row_x.at[my_col], rx_r, {"col": lax.rem(my_col + far, n_col)})
+        peer = lax.rem(my_col + far, n_col)
+        push(x_ref, row_x.at[my_col], rx_r.at[(peer == mirror).astype(jnp.int32)], {"col": peer})
     for peer in others(n_row, my_row):
         push(x_ref, col_x.at[my_row], cx_r, {"row": peer})
     x_own = x_ref[...]
@@ -138,30 +144,61 @@
             part_one[r] = part_one[r] + (place == r).astype(F32) * term
     for r in range(n_col):
         p1_out[r] = part_one[r]
+    if direct:
+        @pl.when(last)
+        def _():
+            for row in range(FAST):
+                push(p1_out.at[0], far_p1.at[my_row], far_r, {"row": row, "col": 0}, far_s)
     for d, peer in enumerate(others(n_col, my_col)):
         push(p1_out.at[peer], p1_in.at[d], p1_r, {"col": peer})
 
     own_diag = diag_ref[...] * x_own
     left = [jnp.concatenate(halves(x_own), axis=0)]
     right = [jnp.concatenate(halves(own_diag), axis=0)]
-    p_two = [jnp.concatenate(halves(part), axis=0) for part in part_one]
-
-    drain(row_x.at[pl.ds(0, n_col - 1)], rx_r)
-    for at in range(n_col):
+    order = [lax.rem(mirror + k, n_col) for k in range(1, n_col)] + [mirror]
+    p_two = [jnp.concatenate(halves(p1_out[at]), axis=0) for at in order]
+
+    def products(left, right):
+        return pack(fold(dot_nt(jnp.concatenate(left, axis=1), jnp.concatenate(right, axis=1))))
+
+    def take(at, p_at):
         both = jnp.concatenate(halves(row_x[at]), axis=0)
         row_lhs[at] = both
-        left += [both, p_two[at]]
-        right += [p_two[at], both]
-    packed = pack(fold(dot_nt(jnp.concatenate(left, axis=1), jnp.concatenate(right, axis=1))))
-    if direct:
-        me = my_col * n_row + my_row
-        g1_in[me] = packed
-        for at in range(n_row * n_col - 1):
+        return [both, p_at], [p_at, both]
+
+    def spread_out(ats, me):
+        for at in ats:
             to = at + (at >= me).astype(jnp.int32)
             push(
                 g1_in.at[me], g1_in.at[me], g1_r,
                 {"row": lax.rem(to, n_row), "col": to // n_row},
             )
+
+    me = my_col * n_row + my_row
+    drain(row_x.at[pl.ds(0, n_col - 2)], rx_r.at[0])
+    for at, p_at in zip(order[:-1], p_two):
+        one, two = take(at, p_at)
+        left += one
+        right += two
+    packed = products(left, right)
+    if direct:
+        far_g[...] = packed
+
+        @pl.when(last)
+        def _():
+            for row in range(FAST):
+                push(far_g, g1_in.at[me], g1_r, {"row": row, "col": 0})
+
+    drain(row_x.at[pl.ds(0, 1)], rx_r.at[1])
+    packed = packed + products(*take(mirror, p_two[-1]))
+    if direct:
+        g1_in[me] = packed
+
+        @pl.when(jnp.logical_not(last))
+        def _():
+            spread_out(range(FAST), me)
+
+        spread_out(range(FAST, n_row * n_col - 1), me)
     else:
         g1_out[...] = packed
         for d, peer in enumerate(others(n_row, my_row)):
@@ -215,8 +252,21 @@
     out_ref[0] = image
 
     if direct:
+        far_sum[...] = jnp.zeros_like(far_sum)
+
+        @pl.when(first)
+        def _():
+            drain(far_p1, far_r)
+            far_left, far_right = [], []
+            for row in range(n_row):
+                both = jnp.concatenate(halves(col_x[row]), axis=0)
+                p_far = jnp.concatenate(halves(far_p1[row]), axis=0)
+                far_left += [both, p_far]
+                far_right += [p_far, both]
+            far_sum[...] = products(far_left, far_right)
+
         drain(g1_in.at[pl.ds(0, n_row * n_col - 1)], g1_r)
-        gram = add([g1_in[d] for d in range(n_row * n_col)])
+        gram = add([far_sum[...]] + [g1_in[d] for d in range(n_row * n_col)])
     else:
         drain(g2_in.at[pl.ds(0, n_col - 1)], g2_r)
         gram = add([g2_out[...]] + [g2_in[d] for d in range(n_col - 1)])
@@ -224,6 +274,10 @@
     o = dot_nn(jnp.concatenate(halves(wide), axis=0), y_two)
     out_ref[1] = image - (o[:count, :BLK] + o[count:, :BLK] + o[:count, BLK:])
     drain(sent, send)
+    if direct:
+        @pl.when(last)
+        def _():
+            drain(far_p1.at[pl.ds(0, FAST)], far_s)
 
 
 def part_kernel(both_ref, image_ref, resid_ref):
@@ -268,8 +322,11 @@
             pltpu.VMEM((groups, BLK), F32),
             pltpu.VMEM((n_col, groups, BLK), F32),
             pltpu.VMEM((8 * pieces + small, groups, BLK), F32),
+            pltpu.VMEM((n_row,) + piece, F32),
+            pltpu.VMEM((groups, BLK), F32),
+            pltpu.VMEM((groups, BLK), F32),
             dma((5,)),
-            dma, dma, dma, dma, dma, dma, dma, dma,
+            dma, dma, dma((2,)), dma, dma, dma, dma, dma, dma, dma,
         ],
         compiler_params=pltpu.CompilerParams(collective_id=0, has_side_effects=True),
     )(vectors, diag_energy.reshape(1, -1), block_row, block_col, blocks)

time: 17 us -> 16.6 us (0.976)
  Pallas kernels: 16.1 us -> 15.7 us
    pallas_call x1, Pallas kernels: 15.5 us -> 15.1 us  [per_device(): pl.pallas_call(functools.partial(kernel, n_row, n_col), out_shape=pltpu.V...]
where the time goes in v2:
time: 16.6 us; the launch traced here: 16.3 us
  Pallas kernels  15.7 us (95%)
  between operations  0.64 us (4%)
    pallas_call x1, Pallas kernels, per_device(): pl.pallas_call(functools.partial(kernel, n_row, n_col), out_shape=pltpu.V...  15.1 us
    pallas_call x1, Pallas kernels, per_device(): pl.pallas_call(part_kernel, out_shape=[jax.ShapeDtypeStruct(piece, F32)]...  0.61 us

profile of v2, /device:TPU:0, one launch (start us, length us, event | category | flops | bytes accessed | tf_op | source)
XLA Modules:
  0.0 16.3 jit_solution(17639116724061598968)
XLA Ops:
  0.6 15.1 %shard_map.68.both_ref = f32[2,16,128]{2,1,0:T(8,128)S(1)} custom-call(f32[16,128]{1,0:T(8,128)} %x_hbm.1, f32[1,128]{1,0:T(1,128)} %bitcast.1, s32[1,24]{1,0:T(1,128)} %rows_hbm.1, s32[1,24]{1,0:T(1,128)} %cols_hbm.1, f32[1,24,128,128]{3,2,1,0:T(8,128)} %blocks_hbm.1), custom_call_target="tpu_custom_call" | custom-call | tf_op jit(solution)/shard_map/pallas_call | solution.py:299
  15.7 0.6 %shard_map.69 = (f32[16,128]{1,0:T(8,128)}, f32[16,128]{1,0:T(8,128)}) custom-call(f32[2,16,128]{2,1,0:T(8,128)S(1)} %shard_map.68.both_ref), custom_call_target="tpu_custom_call" | custom-call | tf_op jit(solution)/shard_map/pallas_call | solution.py:333

commit v3 on v2

--- a/solution.py
+++ b/solution.py
@@ -161,9 +161,8 @@
     def products(left, right):
         return pack(fold(dot_nt(jnp.concatenate(left, axis=1), jnp.concatenate(right, axis=1))))
 
-    def take(at, p_at):
+    def both_ways(at, p_at):
         both = jnp.concatenate(halves(row_x[at]), axis=0)
-        row_lhs[at] = both
         return [both, p_at], [p_at, both]
 
     def spread_out(ats, me):
@@ -176,21 +175,25 @@
 
     me = my_col * n_row + my_row
     drain(row_x.at[pl.ds(0, n_col - 2)], rx_r.at[0])
-    for at, p_at in zip(order[:-1], p_two):
-        one, two = take(at, p_at)
+    if direct:
+        @pl.when(last)
+        def _():
+            some_left, some_right = list(left), list(right)
+            for at, p_at in zip(order[:-1], p_two):
+                one, two = both_ways(at, p_at)
+                some_left += one
+                some_right += two
+            far_g[...] = products(some_left, some_right)
+            for row in range(FAST):
+                push(far_g, g1_in.at[me], g1_r, {"row": row, "col": 0})
+
+    drain(row_x.at[pl.ds(0, 1)], rx_r.at[1])
+    for at, p_at in zip(order, p_two):
+        one, two = both_ways(at, p_at)
+        row_lhs[at] = one[0]
         left += one
         right += two
     packed = products(left, right)
-    if direct:
-        far_g[...] = packed
-
-        @pl.when(last)
-        def _():
-            for row in range(FAST):
-                push(far_g, g1_in.at[me], g1_r, {"row": row, "col": 0})
-
-    drain(row_x.at[pl.ds(0, 1)], rx_r.at[1])
-    packed = packed + products(*take(mirror, p_two[-1]))
     if direct:
         g1_in[me] = packed
 

time: 16.6 us -> 16.3 us (0.982)
  Pallas kernels: 15.7 us -> 15.4 us
    pallas_call x1, Pallas kernels: 15.1 us -> 14.8 us  [per_device(): pl.pallas_call(functools.partial(kernel, n_row, n_col), out_shape=pltpu.V...]
where the time goes in v3:
time: 16.3 us; the launch traced here: 16.1 us
  Pallas kernels  15.4 us (94%)
  between operations  0.64 us (4%)
    pallas_call x1, Pallas kernels, per_device(): pl.pallas_call(functools.partial(kernel, n_row, n_col), out_shape=pltpu.V...  14.8 us
    pallas_call x1, Pallas kernels, per_device(): pl.pallas_call(part_kernel, out_shape=[jax.ShapeDtypeStruct(piece, F32)]...  0.61 us

profile of v3, /device:TPU:0, one launch (start us, length us, event | category | flops | bytes accessed | tf_op | source)
XLA Modules:
  0.0 16.1 jit_solution(7284850751223901900)
XLA Ops:
  0.6 14.8 %shard_map.68.both_ref = f32[2,16,128]{2,1,0:T(8,128)S(1)} custom-call(f32[16,128]{1,0:T(8,128)} %x_hbm.1, f32[1,128]{1,0:T(1,128)} %bitcast.1, s32[1,24]{1,0:T(1,128)} %rows_hbm.1, s32[1,24]{1,0:T(1,128)} %cols_hbm.1, f32[1,24,128,128]{3,2,1,0:T(8,128)} %blocks_hbm.1), custom_call_target="tpu_custom_call" | custom-call | tf_op jit(solution)/shard_map/pallas_call | solution.py:302
  15.5 0.6 %shard_map.69 = (f32[16,128]{1,0:T(8,128)}, f32[16,128]{1,0:T(8,128)}) custom-call(f32[2,16,128]{2,1,0:T(8,128)S(1)} %shard_map.68.both_ref), custom_call_target="tpu_custom_call" | custom-call | tf_op jit(solution)/shard_map/pallas_call | solution.py:336

commit v4 on v2

--- a/solution.py
+++ b/solution.py
@@ -43,8 +43,8 @@
     x_hbm, diag_hbm, rows_hbm, cols_hbm, blocks_hbm,
     out_ref,
     x_ref, diag_ref, rows_ref, cols_ref, tiles, split, col_x, row_x, col_lhs, row_lhs,
-    met_in, p1_out, p1_in, p2_out, p2_in, g1_out, g1_in, g2_out, g2_in, sent, far_p1, far_g, far_sum,
-    load_sem, send, cx_r, rx_r, m_r, p1_r, p2_r, g1_r, g2_r, far_s, far_r,
+    met_in, p1_out, p2_out, p_in, g1_out, g1_in, g2_out, g2_in, sent, far_p1, far_g, far_sum,
+    load_sem, cx_r, rx_r, m_r, p_r, g1_r, far_r, *g2_r,
 ):
     count = x_ref.shape[0]
     n_blk = tiles.shape[0]
@@ -52,6 +52,7 @@
     my_col = lax.axis_index("col")
     direct = n_row * n_col <= DIRECT
 
+    send, far_s = load_sem.at[0], load_sem.at[1]
     last = my_col == n_col - 1
     first = (my_col == 0) & (my_row < FAST)
 
@@ -83,11 +84,15 @@
     pl.semaphore_wait(barrier, n_row + n_col - 2)
 
     mirror = n_col - 1 - my_col
-    upper = my_col // (n_col // 2)
-    for at in range(1, n_col):
-        far = upper * at + (1 - upper) * (n_col - at)
-        peer = lax.rem(my_col + far, n_col)
-        push(x_ref, row_x.at[my_col], rx_r.at[(peer == mirror).astype(jnp.int32)], {"col": peer})
+    half = n_col // 2
+    upper = my_col // half
+    skip = (my_col == 0).astype(jnp.int32)
+    for at in range(n_col - 1):
+        if at < half:
+            peer = upper * at + (1 - upper) * (n_col - 1 - lax.rem(at + skip, half))
+        else:
+            peer = upper * half + lax.rem(my_col + 1 + at - half, half)
+        push(x_ref, row_x.at[my_col], rx_r.at[(0 if at >= half else 1) + (peer == mirror).astype(jnp.int32)], {"col": peer})
     for peer in others(n_row, my_row):
         push(x_ref, col_x.at[my_row], cx_r, {"row": peer})
     x_own = x_ref[...]
@@ -106,11 +111,11 @@
     sub = lax.broadcasted_iota(jnp.int32, (count, BLK), 0)
     keep = (lane // count) == (sub % per)
 
-    def fold(o):
-        return o[:count, :count] + o[count:, :count] + o[:count, count:]
-
-    def pack(square):
-        spread = jnp.where(keep, jnp.concatenate([square] * per, axis=1), 0.0)
+    def pack(o):
+        wide = jnp.concatenate([o[:count], jnp.zeros((count, BLK - 2 * count), F32)], axis=1)
+        wide = wide + jnp.concatenate([o[count:, :count], jnp.zeros((count, BLK - count), F32)], axis=1)
+        spread = add([wide] + [pltpu.roll(wide, count * at, 1) for at in range(1, per)])
+        spread = jnp.where(keep, spread, 0.0)
         return jnp.concatenate(
             [jnp.sum(spread[g * per:(g + 1) * per], axis=0, keepdims=True) for g in range(groups)], axis=0
         )
@@ -131,12 +136,13 @@
         )
         col_two.append(jnp.concatenate([high, low], axis=0))
     x_wide = jnp.concatenate(col_two, axis=1)
-    met_in[my_col] = pack(fold(dot_nt(x_wide, x_wide)))
-    for peer in others(n_col, my_col):
-        push(met_in.at[my_col], met_in.at[my_col], m_r, {"col": peer})
+    met_in[my_col] = pack((dot_nt(x_wide, x_wide)))
 
     part_one = [jnp.zeros((count, BLK), F32) for _ in range(n_col)]
     for b in range(n_blk):
+        if b == n_blk // 3:
+            for peer in others(n_col, my_col):
+                push(met_in.at[my_col], met_in.at[my_col], m_r, {"col": peer})
         o = dot_nt(col_lhs[cols_ref[0, b]], split[b])
         term = o[:count] + o[count:]
         place = rows_ref[0, b]
@@ -150,21 +156,18 @@
             for row in range(FAST):
                 push(p1_out.at[0], far_p1.at[my_row], far_r, {"row": row, "col": 0}, far_s)
     for d, peer in enumerate(others(n_col, my_col)):
-        push(p1_out.at[peer], p1_in.at[d], p1_r, {"col": peer})
+        push(p1_out.at[peer], p_in.at[d], p_r, {"col": peer})
 
     own_diag = diag_ref[...] * x_own
     left = [jnp.concatenate(halves(x_own), axis=0)]
     right = [jnp.concatenate(halves(own_diag), axis=0)]
-    order = [lax.rem(mirror + k, n_col) for k in range(1, n_col)] + [mirror]
+    near = [upper * half + at for at in range(half)]
+    far = [(1 - upper) * half + lax.rem(mirror + at, half) for at in range(1, half)]
+    order = near + far + [mirror]
     p_two = [jnp.concatenate(halves(p1_out[at]), axis=0) for at in order]
 
     def products(left, right):
-        return pack(fold(dot_nt(jnp.concatenate(left, axis=1), jnp.concatenate(right, axis=1))))
-
-    def take(at, p_at):
-        both = jnp.concatenate(halves(row_x[at]), axis=0)
-        row_lhs[at] = both
-        return [both, p_at], [p_at, both]
+        return dot_nt(jnp.concatenate(left, axis=1), jnp.concatenate(right, axis=1))
 
     def spread_out(ats, me):
         for at in ats:
@@ -175,22 +178,31 @@
             )
 
     me = my_col * n_row + my_row
-    drain(row_x.at[pl.ds(0, n_col - 2)], rx_r.at[0])
-    for at, p_at in zip(order[:-1], p_two):
-        one, two = take(at, p_at)
-        left += one
-        right += two
-    packed = products(left, right)
-    if direct:
-        far_g[...] = packed
-
+    def gathered(some):
+        left, right = [], []
+        for at, p_at in some:
+            both = jnp.concatenate(halves(row_x[at]), axis=0)
+            left += [both, p_at]
+            right += [p_at, both]
+        return left, right
+
+    pairs = list(zip(order, p_two))
+    drain(row_x.at[pl.ds(0, half - 1)], rx_r.at[0])
+    one, two = gathered(pairs[:half])
+    near_sum = products(left + one, right + two)
+    for at, both in zip(near, one[::2]):
+        row_lhs[at] = both
+    drain(row_x.at[pl.ds(0, half - 1)], rx_r.at[1])
+    if direct:
         @pl.when(last)
         def _():
+            far_g[...] = pack(near_sum + products(*gathered(pairs[half:-1])))
             for row in range(FAST):
                 push(far_g, g1_in.at[me], g1_r, {"row": row, "col": 0})
 
-    drain(row_x.at[pl.ds(0, 1)], rx_r.at[1])
-    packed = packed + products(*take(mirror, p_two[-1]))
+    drain(row_x.at[pl.ds(0, 1)], rx_r.at[2])
+    one, two = gathered(pairs[half:])
+    packed = pack(near_sum + products(one, two))
     if direct:
         g1_in[me] = packed
 
@@ -203,6 +215,9 @@
         g1_out[...] = packed
         for d, peer in enumerate(others(n_row, my_row)):
             push(g1_out, g1_in.at[d], g1_r, {"row": peer})
+
+    for at, both in zip(order[half:], one[::2]):
+        row_lhs[at] = both
 
     part_two = [jnp.zeros((count, BLK), F32) for _ in range(n_row)]
     for b in range(n_blk):
@@ -214,13 +229,13 @@
     for q in range(n_row):
         p2_out[q] = part_two[q]
     for d, peer in enumerate(others(n_row, my_row)):
-        push(p2_out.at[peer], p2_in.at[d], p2_r, {"row": peer})
+        push(p2_out.at[peer], p_in.at[n_col - 1 + d], p_r, {"row": peer})
 
     if not direct:
         drain(g1_in.at[pl.ds(0, n_row - 1)], g1_r)
         g2_out[...] = add([g1_out[...]] + [g1_in[d] for d in range(n_row - 1)])
         for d, peer in enumerate(others(n_col, my_col)):
-            push(g2_out, g2_in.at[d], g2_r, {"col": peer})
+            push(g2_out, g2_in.at[d], g2_r[0], {"col": peer})
 
     drain(met_in.at[pl.ds(0, n_col - 1)], m_r)
     metric = unpack(add([met_in[d] for d in range(n_col)]))
@@ -243,12 +258,11 @@
         [jnp.concatenate([high] * per, axis=0), jnp.concatenate([low] * per, axis=0)], axis=1
     )
 
-    drain(p2_in.at[pl.ds(0, n_row - 1)], p2_r)
+    drain(p_in, p_r)
     image = own_diag + p2_out[my_row]
     for d in range(n_row - 1):
-        image = image + p2_in[d]
-    drain(p1_in.at[pl.ds(0, n_col - 1)], p1_r)
-    image = add([image, p1_out[my_col]] + [p1_in[d] for d in range(n_col - 1)])
+        image = image + p_in[n_col - 1 + d]
+    image = add([image, p1_out[my_col]] + [p_in[d] for d in range(n_col - 1)])
     out_ref[0] = image
 
     if direct:
@@ -263,12 +277,12 @@
                 p_far = jnp.concatenate(halves(far_p1[row]), axis=0)
                 far_left += [both, p_far]
                 far_right += [p_far, both]
-            far_sum[...] = products(far_left, far_right)
+            far_sum[...] = pack(products(far_left, far_right))
 
         drain(g1_in.at[pl.ds(0, n_row * n_col - 1)], g1_r)
         gram = add([far_sum[...]] + [g1_in[d] for d in range(n_row * n_col)])
     else:
-        drain(g2_in.at[pl.ds(0, n_col - 1)], g2_r)
+        drain(g2_in.at[pl.ds(0, n_col - 1)], g2_r[0])
         gram = add([g2_out[...]] + [g2_in[d] for d in range(n_col - 1)])
     wide = unpack(gram)
     o = dot_nn(jnp.concatenate(halves(wide), axis=0), y_two)
@@ -314,9 +328,8 @@
             pltpu.VMEM((n_col, 2 * count, BLK), BF16),
             pltpu.VMEM((n_col, groups, BLK), F32),
             pltpu.VMEM((n_col,) + piece, F32),
-            pltpu.VMEM((n_col - 1,) + piece, F32),
             pltpu.VMEM((n_row,) + piece, F32),
-            pltpu.VMEM((n_row - 1,) + piece, F32),
+            pltpu.VMEM((n_col + n_row - 2,) + piece, F32),
             pltpu.VMEM((groups, BLK), F32),
             pltpu.VMEM((n_all, groups, BLK), F32),
             pltpu.VMEM((groups, BLK), F32),
@@ -326,7 +339,8 @@
             pltpu.VMEM((groups, BLK), F32),
             pltpu.VMEM((groups, BLK), F32),
             dma((5,)),
-            dma, dma, dma((2,)), dma, dma, dma, dma, dma, dma, dma,
+            dma, dma((3,)), dma, dma, dma, dma,
+            *([] if direct else [dma]),
         ],
         compiler_params=pltpu.CompilerParams(collective_id=0, has_side_effects=True),
     )(vectors, diag_energy.reshape(1, -1), block_row, block_col, blocks)

time: 16.6 us -> 16.1 us (0.970)
  Pallas kernels: 15.7 us -> 15.2 us
    pallas_call x1, Pallas kernels: 15.1 us -> 14.6 us  [per_device(): pl.pallas_call(functools.partial(kernel, n_row, n_col), out_shape=pltpu.V...]
where the time goes in v4:
time: 16.1 us; the launch traced here: 15.9 us
  Pallas kernels  15.2 us (94%)
  between operations  0.64 us (4%)
    pallas_call x1, Pallas kernels, per_device(): pl.pallas_call(functools.partial(kernel, n_row, n_col), out_shape=pltpu.V...  14.6 us
    pallas_call x1, Pallas kernels, per_device(): pl.pallas_call(part_kernel, out_shape=[jax.ShapeDtypeStruct(piece, F32)]...  0.61 us

profile of v4, /device:TPU:0, one launch (start us, length us, event | category | flops | bytes accessed | tf_op | source)
XLA Modules:
  0.0 15.9 jit_solution(14582004383345379586)
XLA Ops:
  0.6 14.6 %shard_map.68.both_ref = f32[2,16,128]{2,1,0:T(8,128)S(1)} custom-call(f32[16,128]{1,0:T(8,128)} %x_hbm.1, f32[1,128]{1,0:T(1,128)} %bitcast.1, s32[1,24]{1,0:T(1,128)} %rows_hbm.1, s32[1,24]{1,0:T(1,128)} %cols_hbm.1, f32[1,24,128,128]{3,2,1,0:T(8,128)} %blocks_hbm.1), custom_call_target="tpu_custom_call" | custom-call | tf_op jit(solution)/shard_map/pallas_call | solution.py:313
  15.3 0.6 %shard_map.69 = (f32[16,128]{1,0:T(8,128)}, f32[16,128]{1,0:T(8,128)}) custom-call(f32[2,16,128]{2,1,0:T(8,128)S(1)} %shard_map.68.both_ref), custom_call_target="tpu_custom_call" | custom-call | tf_op jit(solution)/shard_map/pallas_call | solution.py:347

commit v5 on v4

--- a/solution.py
+++ b/solution.py
@@ -42,11 +42,12 @@
     n_row, n_col,
     x_hbm, diag_hbm, rows_hbm, cols_hbm, blocks_hbm,
     out_ref,
-    x_ref, diag_ref, rows_ref, cols_ref, tiles, split, col_x, row_x, col_lhs, row_lhs,
+    own, where, tiles, split, col_x, row_x, col_lhs, row_lhs,
     met_in, p1_out, p2_out, p_in, g1_out, g1_in, g2_out, g2_in, sent, far_p1, far_g, far_sum,
     load_sem, cx_r, rx_r, m_r, p_r, g1_r, far_r, *g2_r,
 ):
-    count = x_ref.shape[0]
+    count = x_hbm.shape[0]
+    x_ref = own.at[pl.ds(0, count)]
     n_blk = tiles.shape[0]
     my_row = lax.axis_index("row")
     my_col = lax.axis_index("col")
@@ -63,24 +64,22 @@
         ).start()
 
     def others(size, me):
-        return [lax.rem(me + d, size) for d in range(1, size)]
+        if size & (size - 1):
+            return [lax.rem(me + d, size) for d in range(1, size)]
+        return [(me + d) & (size - 1) for d in range(1, size)]
 
     barrier = pltpu.get_barrier_semaphore()
+    for peer in others(n_row, my_row):
+        pl.semaphore_signal(barrier, inc=1, device_id={"row": peer}, device_id_type=MESH)
     for peer in others(n_col, my_col):
         pl.semaphore_signal(barrier, inc=1, device_id={"col": peer}, device_id_type=MESH)
-    for peer in others(n_row, my_row):
-        pl.semaphore_signal(barrier, inc=1, device_id={"row": peer}, device_id_type=MESH)
-
-    x_load, *small_loads, load = [
-        pltpu.make_async_copy(source, target, load_sem.at[at])
-        for at, (source, target) in enumerate(
-            [(x_hbm, x_ref), (diag_hbm, diag_ref), (rows_hbm, rows_ref), (cols_hbm, cols_ref),
-             (blocks_hbm.at[0], tiles)]
-        )
-    ]
-    for copy in [x_load, *small_loads, load]:
-        copy.start()
-    x_load.wait()
+
+    for source, target, at in [
+        (x_hbm, x_ref, 0), (diag_hbm, own.at[pl.ds(count, 1)], 0),
+        (rows_hbm, where.at[pl.ds(0, 1)], 1), (cols_hbm, where.at[pl.ds(1, 1)], 1), (blocks_hbm.at[0], tiles, 2),
+    ]:
+        pltpu.make_async_copy(source, target, load_sem.at[at]).start()
+    drain(own.at[pl.ds(0, count + 1)], load_sem.at[0])
     pl.semaphore_wait(barrier, n_row + n_col - 2)
 
     mirror = n_col - 1 - my_col
@@ -99,8 +98,8 @@
     row_x[my_col] = x_own
     col_x[my_row] = x_own
 
-    for copy in [*small_loads, load]:
-        copy.wait()
+    drain(where, load_sem.at[1])
+    drain(tiles, load_sem.at[2])
     for b in range(n_blk):
         high, low = halves(tiles[b])
         split[b] = jnp.concatenate([high, low], axis=1)
@@ -143,9 +142,9 @@
         if b == n_blk // 3:
             for peer in others(n_col, my_col):
                 push(met_in.at[my_col], met_in.at[my_col], m_r, {"col": peer})
-        o = dot_nt(col_lhs[cols_ref[0, b]], split[b])
+        o = dot_nt(col_lhs[where[1, b]], split[b])
         term = o[:count] + o[count:]
-        place = rows_ref[0, b]
+        place = where[0, b]
         for r in range(n_col):
             part_one[r] = part_one[r] + (place == r).astype(F32) * term
     for r in range(n_col):
@@ -158,7 +157,7 @@
     for d, peer in enumerate(others(n_col, my_col)):
         push(p1_out.at[peer], p_in.at[d], p_r, {"col": peer})
 
-    own_diag = diag_ref[...] * x_own
+    own_diag = own[count:count + 1] * x_own
     left = [jnp.concatenate(halves(x_own), axis=0)]
     right = [jnp.concatenate(halves(own_diag), axis=0)]
     near = [upper * half + at for at in range(half)]
@@ -221,9 +220,9 @@
 
     part_two = [jnp.zeros((count, BLK), F32) for _ in range(n_row)]
     for b in range(n_blk):
-        o = dot_nn(row_lhs[rows_ref[0, b]], split[b])
+        o = dot_nn(row_lhs[where[0, b]], split[b])
         term = o[:count, :BLK] + o[count:, :BLK] + o[:count, BLK:]
-        place = cols_ref[0, b]
+        place = where[1, b]
         for q in range(n_row):
             part_two[q] = part_two[q] + (place == q).astype(F32) * term
     for q in range(n_row):
@@ -270,10 +269,10 @@
 
         @pl.when(first)
         def _():
+            col_both = [jnp.concatenate(halves(col_x[row]), axis=0) for row in range(n_row)]
             drain(far_p1, far_r)
             far_left, far_right = [], []
-            for row in range(n_row):
-                both = jnp.concatenate(halves(col_x[row]), axis=0)
+            for row, both in enumerate(col_both):
                 p_far = jnp.concatenate(halves(far_p1[row]), axis=0)
                 far_left += [both, p_far]
                 far_right += [p_far, both]
@@ -316,10 +315,8 @@
         in_specs=[pl.BlockSpec(memory_space=pl.ANY)] * 5,
         out_specs=vmem,
         scratch_shapes=[
-            pltpu.VMEM(piece, F32),
-            pltpu.VMEM((1, BLK), F32),
-            pltpu.SMEM((1, n_blk), jnp.int32),
-            pltpu.SMEM((1, n_blk), jnp.int32),
+            pltpu.VMEM((count + 8, BLK), F32),
+            pltpu.SMEM((2, n_blk), jnp.int32),
             pltpu.VMEM((n_blk, BLK, BLK), F32),
             pltpu.VMEM((n_blk, BLK, 2 * BLK), BF16),
             pltpu.VMEM((n_row,) + piece, F32),
@@ -338,7 +335,7 @@
             pltpu.VMEM((n_row,) + piece, F32),
             pltpu.VMEM((groups, BLK), F32),
             pltpu.VMEM((groups, BLK), F32),
-            dma((5,)),
+            dma((3,)),
             dma, dma((3,)), dma, dma, dma, dma,
             *([] if direct else [dma]),
         ],

time: 16.1 us -> 16.1 us (level)
  no operation moved by 1% of the time
where the time goes in v5:
time: 16.1 us; the launch traced here: 15.9 us
  Pallas kernels  15.2 us (94%)
  between operations  0.64 us (4%)
    pallas_call x1, Pallas kernels, per_device(): pl.pallas_call(functools.partial(kernel, n_row, n_col), out_shape=pltpu.V...  14.6 us
    pallas_call x1, Pallas kernels, per_device(): pl.pallas_call(part_kernel, out_shape=[jax.ShapeDtypeStruct(piece, F32)]...  0.61 us

profile of v5, /device:TPU:0, one launch (start us, length us, event | category | flops | bytes accessed | tf_op | source)
XLA Modules:
  0.0 15.9 jit_solution(14651461999316378054)
XLA Ops:
  0.6 14.6 %shard_map.68.both_ref = f32[2,16,128]{2,1,0:T(8,128)S(1)} custom-call(f32[16,128]{1,0:T(8,128)} %x_hbm.1, f32[1,128]{1,0:T(1,128)} %bitcast.1, s32[1,24]{1,0:T(1,128)} %rows_hbm.1, s32[1,24]{1,0:T(1,128)} %cols_hbm.1, f32[1,24,128,128]{3,2,1,0:T(8,128)} %blocks_hbm.1), custom_call_target="tpu_custom_call" | custom-call | tf_op jit(solution)/shard_map/pallas_call | solution.py:312
  15.2 0.6 %shard_map.69 = (f32[16,128]{1,0:T(8,128)}, f32[16,128]{1,0:T(8,128)}) custom-call(f32[2,16,128]{2,1,0:T(8,128)S(1)} %shard_map.68.both_ref), custom_call_target="tpu_custom_call" | custom-call | tf_op jit(solution)/shard_map/pallas_call | solution.py:344

commit v6 on v5

--- a/solution.py
+++ b/solution.py
@@ -80,18 +80,19 @@
     ]:
         pltpu.make_async_copy(source, target, load_sem.at[at]).start()
     drain(own.at[pl.ds(0, count + 1)], load_sem.at[0])
-    pl.semaphore_wait(barrier, n_row + n_col - 2)
-
     mirror = n_col - 1 - my_col
     half = n_col // 2
-    upper = my_col // half
+    upper = (my_col >= half).astype(jnp.int32)
     skip = (my_col == 0).astype(jnp.int32)
-    for at in range(n_col - 1):
-        if at < half:
-            peer = upper * at + (1 - upper) * (n_col - 1 - lax.rem(at + skip, half))
-        else:
-            peer = upper * half + lax.rem(my_col + 1 + at - half, half)
-        push(x_ref, row_x.at[my_col], rx_r.at[(0 if at >= half else 1) + (peer == mirror).astype(jnp.int32)], {"col": peer})
+    base, step = (n_col - 1) * (1 - upper) - skip, 2 * upper - 1
+    across = [base + step * at for at in range(half - 1)] + [base + step * (half - 1) + half * skip]
+    beside = [upper * half + ((my_col + at) & (half - 1)) for at in range(1, half)]
+    pl.semaphore_wait(barrier, n_row + n_col - 2)
+
+    for peer in across:
+        push(x_ref, row_x.at[my_col], rx_r.at[1 + (peer == mirror).astype(jnp.int32)], {"col": peer})
+    for peer in beside:
+        push(x_ref, row_x.at[my_col], rx_r.at[0], {"col": peer})
     for peer in others(n_row, my_row):
         push(x_ref, col_x.at[my_row], cx_r, {"row": peer})
     x_own = x_ref[...]

time: 16.1 us -> 16.1 us (level)
  no operation moved by 1% of the time
where the time goes in v6:
time: 16.1 us; the launch traced here: 15.9 us
  Pallas kernels  15.2 us (94%)
  between operations  0.64 us (4%)
    pallas_call x1, Pallas kernels, per_device(): pl.pallas_call(functools.partial(kernel, n_row, n_col), out_shape=pltpu.V...  14.6 us
    pallas_call x1, Pallas kernels, per_device(): pl.pallas_call(part_kernel, out_shape=[jax.ShapeDtypeStruct(piece, F32)]...  0.61 us

profile of v6, /device:TPU:0, one launch (start us, length us, event | category | flops | bytes accessed | tf_op | source)
XLA Modules:
  0.0 15.9 jit_solution(16862774821899834545)
XLA Ops:
  0.6 14.6 %shard_map.68.both_ref = f32[2,16,128]{2,1,0:T(8,128)S(1)} custom-call(f32[16,128]{1,0:T(8,128)} %x_hbm.1, f32[1,128]{1,0:T(1,128)} %bitcast.1, s32[1,24]{1,0:T(1,128)} %rows_hbm.1, s32[1,24]{1,0:T(1,128)} %cols_hbm.1, f32[1,24,128,128]{3,2,1,0:T(8,128)} %blocks_hbm.1), custom_call_target="tpu_custom_call" | custom-call | tf_op jit(solution)/shard_map/pallas_call | solution.py:313
  15.2 0.6 %shard_map.69 = (f32[16,128]{1,0:T(8,128)}, f32[16,128]{1,0:T(8,128)}) custom-call(f32[2,16,128]{2,1,0:T(8,128)S(1)} %shard_map.68.both_ref), custom_call_target="tpu_custom_call" | custom-call | tf_op jit(solution)/shard_map/pallas_call | solution.py:345

commit v7 on v6

--- a/solution.py
+++ b/solution.py
@@ -258,13 +258,6 @@
         [jnp.concatenate([high] * per, axis=0), jnp.concatenate([low] * per, axis=0)], axis=1
     )
 
-    drain(p_in, p_r)
-    image = own_diag + p2_out[my_row]
-    for d in range(n_row - 1):
-        image = image + p_in[n_col - 1 + d]
-    image = add([image, p1_out[my_col]] + [p_in[d] for d in range(n_col - 1)])
-    out_ref[0] = image
-
     if direct:
         far_sum[...] = jnp.zeros_like(far_sum)
 
@@ -279,6 +272,14 @@
                 far_right += [p_far, both]
             far_sum[...] = pack(products(far_left, far_right))
 
+    drain(p_in, p_r)
+    image = own_diag + p2_out[my_row]
+    for d in range(n_row - 1):
+        image = image + p_in[n_col - 1 + d]
+    image = add([image, p1_out[my_col]] + [p_in[d] for d in range(n_col - 1)])
+    out_ref[0] = image
+
+    if direct:
         drain(g1_in.at[pl.ds(0, n_row * n_col - 1)], g1_r)
         gram = add([far_sum[...]] + [g1_in[d] for d in range(n_row * n_col)])
     else:

time: 16.1 us -> 16.1 us (level)
  no operation moved by 1% of the time
where the time goes in v7:
time: 16.1 us; the launch traced here: 15.9 us
  Pallas kernels  15.2 us (94%)
  between operations  0.64 us (4%)
    pallas_call x1, Pallas kernels, per_device(): pl.pallas_call(functools.partial(kernel, n_row, n_col), out_shape=pltpu.V...  14.6 us
    pallas_call x1, Pallas kernels, per_device(): pl.pallas_call(part_kernel, out_shape=[jax.ShapeDtypeStruct(piece, F32)]...  0.61 us

profile of v7, /device:TPU:0, one launch (start us, length us, event | category | flops | bytes accessed | tf_op | source)
XLA Modules:
  0.0 15.9 jit_solution(7929464816720658498)
XLA Ops:
  0.6 14.6 %shard_map.68.both_ref = f32[2,16,128]{2,1,0:T(8,128)S(1)} custom-call(f32[16,128]{1,0:T(8,128)} %x_hbm.1, f32[1,128]{1,0:T(1,128)} %bitcast.1, s32[1,24]{1,0:T(1,128)} %rows_hbm.1, s32[1,24]{1,0:T(1,128)} %cols_hbm.1, f32[1,24,128,128]{3,2,1,0:T(8,128)} %blocks_hbm.1), custom_call_target="tpu_custom_call" | custom-call | tf_op jit(solution)/shard_map/pallas_call | solution.py:314
  15.2 0.6 %shard_map.69 = (f32[16,128]{1,0:T(8,128)}, f32[16,128]{1,0:T(8,128)}) custom-call(f32[2,16,128]{2,1,0:T(8,128)S(1)} %shard_map.68.both_ref), custom_call_target="tpu_custom_call" | custom-call | tf_op jit(solution)/shard_map/pallas_call | solution.py:346

commit v8 on v7

--- a/solution.py
+++ b/solution.py
@@ -89,12 +89,12 @@
     beside = [upper * half + ((my_col + at) & (half - 1)) for at in range(1, half)]
     pl.semaphore_wait(barrier, n_row + n_col - 2)
 
+    for peer in others(n_row, my_row):
+        push(x_ref, col_x.at[my_row], cx_r, {"row": peer})
     for peer in across:
         push(x_ref, row_x.at[my_col], rx_r.at[1 + (peer == mirror).astype(jnp.int32)], {"col": peer})
     for peer in beside:
         push(x_ref, row_x.at[my_col], rx_r.at[0], {"col": peer})
-    for peer in others(n_row, my_row):
-        push(x_ref, col_x.at[my_row], cx_r, {"row": peer})
     x_own = x_ref[...]
     row_x[my_col] = x_own
     col_x[my_row] = x_own

time: 16.1 us -> 16.1 us (level)
  no operation moved by 1% of the time
where the time goes in v8:
time: 16.1 us; the launch traced here: 15.9 us
  Pallas kernels  15.2 us (94%)
  between operations  0.64 us (4%)
    pallas_call x1, Pallas kernels, per_device(): pl.pallas_call(functools.partial(kernel, n_row, n_col), out_shape=pltpu.V...  14.6 us
    pallas_call x1, Pallas kernels, per_device(): pl.pallas_call(part_kernel, out_shape=[jax.ShapeDtypeStruct(piece, F32)]...  0.61 us

profile of v8, /device:TPU:0, one launch (start us, length us, event | category | flops | bytes accessed | tf_op | source)
XLA Modules:
  0.0 15.9 jit_solution(14243054959276753609)
XLA Ops:
  0.6 14.6 %shard_map.68.both_ref = f32[2,16,128]{2,1,0:T(8,128)S(1)} custom-call(f32[16,128]{1,0:T(8,128)} %x_hbm.1, f32[1,128]{1,0:T(1,128)} %bitcast.1, s32[1,24]{1,0:T(1,128)} %rows_hbm.1, s32[1,24]{1,0:T(1,128)} %cols_hbm.1, f32[1,24,128,128]{3,2,1,0:T(8,128)} %blocks_hbm.1), custom_call_target="tpu_custom_call" | custom-call | tf_op jit(solution)/shard_map/pallas_call | solution.py:314
  15.2 0.6 %shard_map.69 = (f32[16,128]{1,0:T(8,128)}, f32[16,128]{1,0:T(8,128)}) custom-call(f32[2,16,128]{2,1,0:T(8,128)S(1)} %shard_map.68.both_ref), custom_call_target="tpu_custom_call" | custom-call | tf_op jit(solution)/shard_map/pallas_call | solution.py:346
